TPU v7x, 32 devices: a whole 2x2x4 slice. The times are simulated.
32 devices in a mesh: row: 2 (over x), col: 4 (over z), depth: 4 (over y, core).
Axes of the slice: x: 2, y: 2, z: 4, core: 2. Of those that a mesh axis runs over, the one named last changes fastest.
Arguments:
- trailing: float32 [8192, 8192], P('row', 'col'), may hold values from -6 to 6
- panel: bfloat16 [8192, 4096], P('row', 'col'), may hold values from -0.75 to 0.75
- inverse_factor: bfloat16 [4096, 4096], P('depth', 'col'), may hold values from -0.09375 to 0.09375
- block_inverse: float32 [8192, 512], P('row'), may hold values from -0.25 to 0.25
- guess: float32 [8192, 128], P(('col', 'depth')), may hold values from -0.0625 to 0.0625
- target: float32 [8192, 128], P('row'), may hold values from -6 to 6
Outputs:
- updated: float32 [8192, 8192], P('row', ('col', 'depth'))
- correction: float32 [8192, 128], P('row')
- residual_rms: float32 [1], replicated
All inputs are finite; a program needn't handle non-finite values.
Results may differ from a plain program's by a relative error of at most 0.00036.
Values may be sent and summed in bfloat16 or wider, within the bound.
A program may use at most 192 MiB of HBM per device.

v0:
```python
import jax
import jax.numpy as jnp
from jax import lax
from jax.sharding import PartitionSpec as P

N = 8192
BS = 512
R = 128


def body(trailing, panel, inverse_factor, block_inverse, guess, target):
    rows_here = panel.shape[0]
    cols_here = trailing.shape[1]
    width_k = inverse_factor.shape[0]
    width_j = inverse_factor.shape[1]
    row_id = lax.axis_index("row")
    col_id = lax.axis_index("col")
    depth_id = lax.axis_index("depth")
    k_index = depth_id * width_k + lax.broadcasted_iota(jnp.int32, (width_k, width_j), 0)
    j_index = col_id * width_j + lax.broadcasted_iota(jnp.int32, (width_k, width_j), 1)
    lower = jnp.where(k_index >= j_index, inverse_factor, jnp.zeros_like(inverse_factor))
    partial_value = lax.dot_general(
        panel, lower, (((1,), (1,)), ((), ())), preferred_element_type=jnp.float32
    )
    share = lax.psum_scatter(partial_value, "col", scatter_dimension=0, tiled=True)
    everything = lax.all_gather(share.astype(jnp.bfloat16), ("row", "col"), axis=0, tiled=True)
    factor_rows = lax.dynamic_slice_in_dim(everything, row_id * rows_here, rows_here, 0)
    factor_cols = lax.dynamic_slice_in_dim(everything, col_id * cols_here, cols_here, 0)
    share_cols = cols_here // lax.axis_size("depth")
    product = lax.dot_general(
        factor_rows, factor_cols, (((1,), (1,)), ((), ())), preferred_element_type=jnp.float32
    )
    total = lax.psum_scatter(product, "depth", scatter_dimension=1, tiled=True)
    mine = lax.dynamic_slice_in_dim(trailing, depth_id * share_cols, share_cols, 1)
    updated = mine - total
    applied = jnp.dot(
        updated, guess, precision=lax.Precision.HIGHEST, preferred_element_type=jnp.float32
    )
    applied = lax.psum(applied, ("col", "depth"))
    residual = target - applied
    squares = lax.psum(jnp.sum(residual * residual), "row")
    residual_rms = jnp.sqrt(squares / (N * R))
    count = rows_here // BS
    blocks = jnp.tril(block_inverse.reshape(count, BS, BS))
    pieces = residual.reshape(count, BS, residual.shape[1])
    first = jnp.einsum("bij,bjr->bir", blocks, pieces, precision=lax.Precision.HIGHEST)
    second = jnp.einsum("bji,bjr->bir", blocks, first, precision=lax.Precision.HIGHEST)
    correction = second.reshape(rows_here, residual.shape[1])
    return (updated, correction, residual_rms.reshape(1))


def solution(mesh):
    placed = (
        P("row", "col"),
        P("row", "col"),
        P("depth", "col"),
        P("row", None),
        P(("col", "depth"), None),
        P("row", None),
    )
    return jax.shard_map(
        body,
        mesh=mesh,
        in_specs=placed,
        out_specs=(P("row", ("col", "depth")), P("row", None), P()),
        check_vma=False,
    )
```

profile of v0, /device:TPU:0, one launch (start us, length us, event | category | flops | bytes accessed | tf_op | source)
XLA Modules:
  0.0 956.3 jit_solution(15078148875091785911)
XLA Ops:
  7.2 0.0 copy-start
  7.2 0.0 reduce-scatter.3.cloned.1.call-start
  7.2 16.3 %convolution_bitcast_fusion = f32[4096,1024]{0,1:T(8,128)} fusion(bf16[4096,1024]{1,0:T(8,128)(2,1)} %param.7, bf16[1024,1024]{1,0:T(8,128)(2,1)} %param.8, s32[1024]{0:T(1024)S(1)} %get-tuple-element.5, s32[1024]{0:T(1024)S(1)} %get-tuple-element.6), kind=kOutput, calls=%fused_computation | convolution fusion | flops 8592031744 | bytes 27271168 | tf_op jit(solution)/shard_map/dot_general | solution.py:22
  23.5 0.0 reduce-scatter.3.cloned.1.call-update
  23.5 0.0 all-gather.2.cloned.1.call-start
  23.6 283.3 %reduce-scatter.3.cloned.1.call-done = f32[1024,1024]{0,1:T(8,128)} async-done(((f32[4096,1024]{0,1:T(8,128)}), f32[1024,1024]{0,1:T(8,128)}) %reduce-scatter.3.cloned.1.call-update) | async-done | bytes 4194320 | tf_op jit(solution)/shard_map/reduce_scatter | solution.py:25
  306.9 3.8 convert_element_type.3
  310.7 0.0 all-gather.2.cloned.1.call-update
  310.7 0.0 reduce-scatter.5.cloned.1.call-start
  310.8 228.0 %all-gather.2.cloned.1.call-done = bf16[8192,1024]{0,1:T(8,128)(2,1)} async-done(((bf16[1024,1024]{0,1:T(8,128)(2,1)}), bf16[8192,1024]{0,1:T(8,128)(2,1)}) %all-gather.2.cloned.1.call-update) | async-done | bytes 16777232 | tf_op jit(solution)/shard_map/all_gather | solution.py:26
  538.8 25.5 %fusion = f32[4096,2048]{1,0:T(8,128)} fusion(bf16[8192,1024]{0,1:T(8,128)(2,1)} %all-gather.2.cloned.1.call-done, s32[]{:T(128)S(6)} %select_n.19, s32[]{:T(128)S(6)} %select_n.20), kind=kOutput, calls=%fused_computation.1 | convolution fusion | flops 17179869184 | bytes 46137352 | tf_op jit(solution)/shard_map/dot_general | solution.py:30
  564.3 0.0 reduce-scatter.5.cloned.1.call-update
  564.3 0.0 all-reduce.2.cloned.1.call-start
  564.4 230.4 %reduce-scatter.5.cloned.1.call-done = f32[4096,512]{1,0:T(8,128)} async-done(((f32[4096,2048]{1,0:T(8,128)}), f32[4096,512]{1,0:T(8,128)}) %reduce-scatter.5.cloned.1.call-update) | async-done | bytes 8388624 | tf_op jit(solution)/shard_map/reduce_scatter | solution.py:33
  794.8 11.3 %dynamic-slice_subtract_fusion = f32[4096,512]{1,0:T(8,128)} fusion(f32[4096,512]{1,0:T(8,128)} %reduce-scatter.5.cloned.1.call-done, f32[4096,2048]{1,0:T(8,128)} %param.6, s32[]{:T(128)S(6)} %select_n.17), kind=kLoop, calls=%fused_computation.3 | loop fusion | flops 2097152 | bytes 25165828 | tf_op jit(solution)/shard_map/sub | solution.py:35
  806.1 0.0 copy-done
  806.1 10.1 %fusion.18 = f32[4096,128]{1,0:T(8,128)} fusion(f32[4096,512]{1,0:T(8,128)} %dynamic-slice_subtract_fusion, f32[512,128]{1,0:T(8,128)S(1)} %copy-done), kind=kOutput, calls=%fused_computation.25 | convolution fusion | flops 3221225472 | bytes 10747904 | tf_op jit(solution)/shard_map/dot_general | solution.py:36
  816.2 0.0 all-reduce.2.cloned.1.call-update
  816.2 0.0 copy-start.1
  816.2 9.3 copy.9
  825.5 0.1 iota_compare_fusion
  825.6 88.8 %all-reduce.2.cloned.1.call-done = f32[4096,128]{1,0:T(8,128)} async-done(((f32[4096,128]{1,0:T(8,128)}), f32[4096,128]{1,0:T(8,128)}) %all-reduce.2.cloned.1.call-update) | async-done | bytes 2097168 | tf_op jit(solution)/shard_map/psum | solution.py:39
  914.4 0.0 copy-done.1
  914.4 0.0 slice-start
  914.4 2.9 multiply_reduce_fusion
  917.3 0.0 slice-start.1
  917.3 16.1 %fusion.4 = f32[8,512,128]{2,1,0:T(8,128)S(1)} fusion(f32[8,512,128]{2,1,0:T(8,128)S(1)} %bitcast.13, f32[8,512,512]{1,2,0:T(8,128)} %copy.9, pred[512,512]{0,1:T(8,128)(4,1)S(1)} %iota_compare_fusion), kind=kOutput, calls=%fused_computation.6 | convolution fusion | flops 3223322624 | bytes 12845056 | tf_op jit(solution)/shard_map/bij,bjr->bir/dot_general | solution.py:46
  933.4 0.0 slice-done
  933.4 0.0 slice-done.1
  933.4 9.0 fusion.2
  942.4 5.5 psum.15
  (2 shorter events, 0.0 us)
Async XLA Ops:
  7.2 798.9 %copy-start = (f32[512,128]{1,0:T(8,128)S(1)}, f32[512,128]{1,0:T(8,128)}, u32[]{:S(2)}) copy-start(f32[512,128]{1,0:T(8,128)} %param.10) | copy-start | bytes 786436
  7.2 299.7 %reduce-scatter.3.cloned.1.call-start = ((), (), s32[]{:S(2)}) async-start(), calls=%async_computation.2 | async-start | bytes 20971520 | tf_op jit(solution)/shard_map/reduce_scatter | solution.py:25
  23.5 515.2 %all-gather.2.cloned.1.call-start = ((), (), s32[]{:S(2)}) async-start(), calls=%async_computation.3 | async-start | bytes 18874368 | tf_op jit(solution)/shard_map/all_gather | solution.py:26
  310.7 484.1 %reduce-scatter.5.cloned.1.call-start = ((), (), s32[]{:S(2)}) async-start(), calls=%async_computation.4 | async-start | bytes 41943040 | tf_op jit(solution)/shard_map/reduce_scatter | solution.py:33
  564.3 350.1 %all-reduce.2.cloned.1.call-start = ((), (), s32[]{:S(2)}) async-start(), calls=%async_computation.5 | async-start | bytes 4194304 | tf_op jit(solution)/shard_map/psum | solution.py:39
  816.2 98.2 %copy-start.1 = (f32[4096,128]{1,0:T(8,128)S(1)}, f32[4096,128]{1,0:T(8,128)}, u32[]{:S(2)}) copy-start(f32[4096,128]{1,0:T(8,128)} %param.11) | copy-start | bytes 6291460
  914.4 19.0 %slice-start = ((s8[8388608]{0:T(1024)(128)(4,1)}), s8[4194304]{0:T(1024)(128)(4,1)S(1)}, s32[]{:S(2)}) async-start(s8[8388608]{0:T(1024)(128)(4,1)} %bitcast.11), calls=%async_computation.6 | async-start | bytes 8388608
  917.3 16.1 %slice-start.1 = ((s8[8388608]{0:T(1024)(128)(4,1)}), s8[4194304]{0:T(1024)(128)(4,1)S(1)}, s32[]{:S(2)}) async-start(s8[8388608]{0:T(1024)(128)(4,1)} %bitcast.11), calls=%async_computation.7 | async-start | bytes 8388608
Sparse Core Ops, SparseCore 0:
  23.7 283.1 reduce-scatter.2
  310.8 227.8 all-gather.1
  564.5 230.3 reduce-scatter.4
  816.3 98.0 all-reduce.1
where the time goes:
time: 957 us; the launch traced here: 956 us
  waiting for transfers between devices  831 us (87%)
  matrix products  77 us (8%)
  other arithmetic  18.1 us (2%)
  between operations  15.7 us (2%)
    reduce_scatter x1, waiting for transfers between devices, body(): lax.psum_scatter(partial_value, 'col', scatter_dimension=0, tiled=True)  283 us
    reduce_scatter x1, waiting for transfers between devices, body(): total = lax.psum_scatter(product, 'depth', scatter_dimension=1, tiled=True)  230 us
    all_gather x1, waiting for transfers between devices, body(): lax.all_gather(share.astype(jnp.bfloat16), ('row', 'col'), axis=0, tiled=...  228 us
    psum x1, waiting for transfers between devices, body(): applied = lax.psum(applied, ('col', 'depth'))  88.8 us
    dot_general x1, matrix products, body(): lax.dot_general(factor_rows, factor_cols, (((1,), (1,)), ((), ())), prefe...  25.5 us
  transfers between devices with their start and end apart: 4, of which 4 were waited for; matrix products, arithmetic and copies ran while one was open for 1% of the time, Pallas kernels for 0%

commit v1 on v0

--- a/solution.py
+++ b/solution.py
@@ -36,7 +36,8 @@
     applied = jnp.dot(
         updated, guess, precision=lax.Precision.HIGHEST, preferred_element_type=jnp.float32
     )
-    applied = lax.psum(applied, ("col", "depth"))
+    for over in ("depth", "col"):
+        applied = lax.psum(applied, over)
     residual = target - applied
     squares = lax.psum(jnp.sum(residual * residual), "row")
     residual_rms = jnp.sqrt(squares / (N * R))

time: 957 us -> 998 us (1.043)
  waiting for transfers between devices: 831 us -> 872 us
    psum x1 -> x2, waiting for transfers between devices: 88.8 us -> 130 us  [body(): applied = lax.psum(applied, over)]
  transfers between devices with their start and end apart: 4 -> 5, of which waited for: 4 -> 5; matrix products, arithmetic and copies ran while one was open for 1% -> 1% of each run, Pallas kernels for 0% -> 0%
where the time goes in v1:
time: 998 us
  waiting for transfers between devices  872 us (87%)
  matrix products  77 us (8%)
  other arithmetic  18.1 us (2%)
  between operations  15.7 us (2%)
    reduce_scatter x1, waiting for transfers between devices, body(): lax.psum_scatter(partial_value, 'col', scatter_dimension=0, tiled=True)  283 us
    reduce_scatter x1, waiting for transfers between devices, body(): total = lax.psum_scatter(product, 'depth', scatter_dimension=1, tiled=True)  230 us
    all_gather x1, waiting for transfers between devices, body(): lax.all_gather(share.astype(jnp.bfloat16), ('row', 'col'), axis=0, tiled=...  228 us
    psum x2, waiting for transfers between devices, body(): applied = lax.psum(applied, over)  130 us
    dot_general x1, matrix products, body(): lax.dot_general(factor_rows, factor_cols, (((1,), (1,)), ((), ())), prefe...  25.5 us
  transfers between devices with their start and end apart: 5, of which 5 were waited for; matrix products, arithmetic and copies ran while one was open for 1% of the time, Pallas kernels for 0%

profile of v1, /device:TPU:0, one launch (start us, length us, event | category | flops | bytes accessed | tf_op | source)
XLA Modules:
  0.0 998.1 jit_solution(12481906959672289504)
XLA Ops:
  7.2 0.0 copy-start
  7.2 0.0 reduce-scatter.3.cloned.1.call-start
  7.2 16.3 %convolution_bitcast_fusion = f32[4096,1024]{0,1:T(8,128)} fusion(bf16[4096,1024]{1,0:T(8,128)(2,1)} %param.7, bf16[1024,1024]{1,0:T(8,128)(2,1)} %param.8, s32[1024]{0:T(1024)S(1)} %get-tuple-element.5, s32[1024]{0:T(1024)S(1)} %get-tuple-element.6), kind=kOutput, calls=%fused_computation | convolution fusion | flops 8592031744 | bytes 27271168 | tf_op jit(solution)/shard_map/dot_general | solution.py:22
  23.5 0.0 reduce-scatter.3.cloned.1.call-update
  23.5 0.0 all-gather.2.cloned.1.call-start
  23.6 283.3 %reduce-scatter.3.cloned.1.call-done = f32[1024,1024]{0,1:T(8,128)} async-done(((f32[4096,1024]{0,1:T(8,128)}), f32[1024,1024]{0,1:T(8,128)}) %reduce-scatter.3.cloned.1.call-update) | async-done | bytes 4194320 | tf_op jit(solution)/shard_map/reduce_scatter | solution.py:25
  306.9 3.8 convert_element_type.3
  310.7 0.0 all-gather.2.cloned.1.call-update
  310.7 0.0 reduce-scatter.5.cloned.1.call-start
  310.8 228.0 %all-gather.2.cloned.1.call-done = bf16[8192,1024]{0,1:T(8,128)(2,1)} async-done(((bf16[1024,1024]{0,1:T(8,128)(2,1)}), bf16[8192,1024]{0,1:T(8,128)(2,1)}) %all-gather.2.cloned.1.call-update) | async-done | bytes 16777232 | tf_op jit(solution)/shard_map/all_gather | solution.py:26
  538.8 25.5 %fusion = f32[4096,2048]{1,0:T(8,128)} fusion(bf16[8192,1024]{0,1:T(8,128)(2,1)} %all-gather.2.cloned.1.call-done, s32[]{:T(128)S(6)} %select_n.19, s32[]{:T(128)S(6)} %select_n.20), kind=kOutput, calls=%fused_computation.1 | convolution fusion | flops 17179869184 | bytes 46137352 | tf_op jit(solution)/shard_map/dot_general | solution.py:30
  564.3 0.0 reduce-scatter.5.cloned.1.call-update
  564.3 0.2 all-reduce.3.cloned.1.call-start
  564.6 230.3 %reduce-scatter.5.cloned.1.call-done = f32[4096,512]{1,0:T(8,128)} async-done(((f32[4096,2048]{1,0:T(8,128)}), f32[4096,512]{1,0:T(8,128)}) %reduce-scatter.5.cloned.1.call-update) | async-done | bytes 8388624 | tf_op jit(solution)/shard_map/reduce_scatter | solution.py:33
  794.8 11.3 %dynamic-slice_subtract_fusion = f32[4096,512]{1,0:T(8,128)} fusion(f32[4096,512]{1,0:T(8,128)} %reduce-scatter.5.cloned.1.call-done, f32[4096,2048]{1,0:T(8,128)} %param.6, s32[]{:T(128)S(6)} %select_n.17), kind=kLoop, calls=%fused_computation.3 | loop fusion | flops 2097152 | bytes 25165828 | tf_op jit(solution)/shard_map/sub | solution.py:35
  806.1 0.0 copy-done
  806.1 10.1 %fusion.18 = f32[4096,128]{1,0:T(8,128)} fusion(f32[4096,512]{1,0:T(8,128)} %dynamic-slice_subtract_fusion, f32[512,128]{1,0:T(8,128)S(1)} %copy-done), kind=kOutput, calls=%fused_computation.25 | convolution fusion | flops 3221225472 | bytes 10747904 | tf_op jit(solution)/shard_map/dot_general | solution.py:36
  816.1 0.0 all-reduce.3.cloned.1.call-update
  816.2 0.3 all-reduce.5.cloned.1.call-start
  816.4 51.3 %all-reduce.3.cloned.1.call-done = f32[4096,128]{1,0:T(8,128)} async-done(((f32[4096,128]{1,0:T(8,128)}), f32[4096,128]{1,0:T(8,128)}) %all-reduce.3.cloned.1.call-update) | async-done | bytes 2097168 | tf_op jit(solution)/shard_map/psum | solution.py:40
  867.7 0.0 all-reduce.5.cloned.1.call-update
  867.7 0.0 copy-start.1
  867.8 9.4 copy.9
  877.1 0.1 iota_compare_fusion
  877.2 78.9 %all-reduce.5.cloned.1.call-done = f32[4096,128]{1,0:T(8,128)} async-done(((f32[4096,128]{1,0:T(8,128)}), f32[4096,128]{1,0:T(8,128)}) %all-reduce.5.cloned.1.call-update) | async-done | bytes 2097168 | tf_op jit(solution)/shard_map/psum | solution.py:40
  956.2 0.0 copy-done.1
  956.2 2.9 multiply_reduce_fusion
  959.1 16.1 %fusion.4 = f32[8,512,128]{2,1,0:T(8,128)S(1)} fusion(f32[8,512,128]{2,1,0:T(8,128)S(1)} %bitcast.13, f32[8,512,512]{1,2,0:T(8,128)} %copy.9, pred[512,512]{0,1:T(8,128)(4,1)S(1)} %iota_compare_fusion), kind=kOutput, calls=%fused_computation.6 | convolution fusion | flops 3223322624 | bytes 12845056 | tf_op jit(solution)/shard_map/bij,bjr->bir/dot_general | solution.py:47
  975.2 0.0 slice-done
  975.2 0.0 slice-done.1
  975.2 9.0 fusion.2
  984.3 5.5 psum.23
  (4 shorter events, 0.0 us)
Async XLA Ops:
  7.2 798.9 %copy-start = (f32[512,128]{1,0:T(8,128)S(1)}, f32[512,128]{1,0:T(8,128)}, u32[]{:S(2)}) copy-start(f32[512,128]{1,0:T(8,128)} %param.10) | copy-start | bytes 786436
  7.2 299.7 %reduce-scatter.3.cloned.1.call-start = ((), (), s32[]{:S(2)}) async-start(), calls=%async_computation.2 | async-start | bytes 20971520 | tf_op jit(solution)/shard_map/reduce_scatter | solution.py:25
  23.5 515.2 %all-gather.2.cloned.1.call-start = ((), (), s32[]{:S(2)}) async-start(), calls=%async_computation.3 | async-start | bytes 18874368 | tf_op jit(solution)/shard_map/all_gather | solution.py:26
  310.7 484.1 %reduce-scatter.5.cloned.1.call-start = ((), (), s32[]{:S(2)}) async-start(), calls=%async_computation.4 | async-start | bytes 41943040 | tf_op jit(solution)/shard_map/reduce_scatter | solution.py:33
  564.3 303.4 %all-reduce.3.cloned.1.call-start = ((), (), s32[]{:S(2)}) async-start(), calls=%async_computation.5 | async-start | bytes 4194304 | tf_op jit(solution)/shard_map/psum | solution.py:40
  816.2 140.0 %all-reduce.5.cloned.1.call-start = ((), (), s32[]{:S(2)}) async-start(), calls=%async_computation.6 | async-start | bytes 4194304 | tf_op jit(solution)/shard_map/psum | solution.py:40
  867.7 88.4 %copy-start.1 = (f32[4096,128]{1,0:T(8,128)S(1)}, f32[4096,128]{1,0:T(8,128)}, u32[]{:S(2)}) copy-start(f32[4096,128]{1,0:T(8,128)} %param.11) | copy-start | bytes 6291460
  956.2 19.0 %slice-start = ((s8[8388608]{0:T(1024)(128)(4,1)}), s8[4194304]{0:T(1024)(128)(4,1)S(1)}, s32[]{:S(2)}) async-start(s8[8388608]{0:T(1024)(128)(4,1)} %bitcast.11), calls=%async_computation.7 | async-start | bytes 8388608
  959.1 16.1 %slice-start.1 = ((s8[8388608]{0:T(1024)(128)(4,1)}), s8[4194304]{0:T(1024)(128)(4,1)S(1)}, s32[]{:S(2)}) async-start(s8[8388608]{0:T(1024)(128)(4,1)} %bitcast.11), calls=%async_computation.8 | async-start | bytes 8388608
Sparse Core Ops, SparseCore 0:
  23.7 283.1 reduce-scatter.2
  310.8 227.8 all-gather.1
  564.5 230.3 reduce-scatter.4
  816.3 51.3 all-reduce.2
  869.9 86.1 all-reduce.4
